TPU v7x, 128 devices: a whole 4x4x4 slice. The times are simulated.
128 devices in a mesh: row: 8 (over z, x_hi), col: 16 (over y, x_lo, core).
Axes of the slice: x: 4 (x_hi: 2, x_lo: 2; x = x_hi * 2 + x_lo), y: 4, z: 4, core: 2. Of those that a mesh axis runs over, the one named last changes fastest.
Arguments:
- features: bfloat16 [32768, 512], P('row'), may hold values from -6 to 6
- logits: float32 [32768, 128], P(('row', 'col')), may hold values from -16 to 16
Outputs:
- memberships: float32 [32768, 128], P(('row', 'col'))
- standardized: float32 [32768, 128], P(('row', 'col'))
All inputs are finite; a program needn't handle non-finite values.
Results may differ from a plain program's by a relative error of at most 0.0003.
Values may be sent and summed in bfloat16 or wider, within the bound.
A program may use at most 64 MiB of HBM per device.

v0:
```python
import math

import jax
import jax.numpy as jnp
from jax import lax
from jax.sharding import PartitionSpec as P

ITERS = 2


def kernel_product(left_rows, right_rows, members):
    count = left_rows.shape[0]
    feature_width = left_rows.shape[1]
    block_rows = math.gcd(count, 512)
    blocks = left_rows.reshape(count // block_rows, block_rows, feature_width)

    def block_product(block):
        inner = jnp.einsum("bf,nf->bn", block, right_rows, preferred_element_type=jnp.float32)
        base = 1.0 + inner / feature_width
        kernel = base * base * base
        return jnp.dot(
            kernel, members, precision=lax.Precision.HIGHEST, preferred_element_type=jnp.float32
        )

    return lax.map(block_product, blocks).reshape(count, members.shape[1])


def on_device(features, logits):
    frames = logits.shape[0]
    column = lax.axis_index("col")
    own_rows = lax.dynamic_slice_in_dim(features, column * frames, frames, 0)
    column_panel = lax.all_gather(own_rows, "row", axis=0, tiled=True)
    raised = jnp.exp(logits)
    members = raised / jnp.sum(raised, axis=1, keepdims=True)
    standardized = members
    for iteration in range(ITERS):
        members_column = lax.all_gather(members, "row", axis=0, tiled=True)
        scores = lax.psum_scatter(
            kernel_product(features, column_panel, members_column),
            "col",
            scatter_dimension=0,
            tiled=True,
        )
        cluster_size, weighted = lax.psum(
            (jnp.sum(members, axis=0), jnp.sum(members * scores, axis=0)), ("row", "col")
        )
        compact = weighted / (cluster_size * cluster_size)
        distance = compact[None, :] - 2.0 * scores / cluster_size[None, :]
        centered = distance - jnp.mean(distance, axis=1, keepdims=True)
        spread = jnp.mean(centered * centered, axis=1, keepdims=True)
        standardized = centered / jnp.sqrt(spread + 1e-06)
        raised = jnp.exp(-2.0 * standardized)
        members = raised / jnp.sum(raised, axis=1, keepdims=True)
    return (members, standardized)


def solution(mesh):
    return jax.shard_map(
        on_device,
        mesh=mesh,
        in_specs=(P("row", None), P(("row", "col"), None)),
        out_specs=(P(("row", "col"), None), P(("row", "col"), None)),
        check_vma=False,
    )
```

profile of v0, /device:TPU:1, one launch (start us, length us, event | category | flops | bytes accessed | tf_op | source)
XLA Modules:
  0.0 545.2 jit_solution(2299477837792060629)
XLA Ops:
  8.2 1.7 exponential_divide_fusion
  10.0 1.7 constant_dynamic-slice_fusion
  11.7 47.2 %all-gather.6.cloned.1.call-done = f32[2048,128]{1,0:T(8,128)} async-done(((f32[256,128]{1,0:T(8,128)}), f32[2048,128]{1,0:T(8,128)}) %all-gather.6.cloned.1.call-update) | async-done | bytes 1048592 | tf_op jit(solution)/shard_map/all_gather | solution.py:37
  59.0 55.7 %all-gather.4.cloned.1.call-done = bf16[2048,512]{1,0:T(8,128)(2,1)} async-done(((bf16[256,512]{1,0:T(8,128)(2,1)}), bf16[2048,512]{1,0:T(8,128)(2,1)}) %all-gather.4.cloned.1.call-update) | async-done | bytes 2097168 | tf_op jit(solution)/shard_map/all_gather | solution.py:32
  114.8 54.8 %while.20 = (s32[]{:T(128)}, f32[8,512,128]{2,1,0:T(8,128)S(1)}, bf16[8,512,512]{2,1,0:T(8,128)(2,1)}, bf16[2048,512]{1,0:T(8,128)(2,1)}, f32[2048,128]{1,0:T(8,128)}, /*index=5*/s32[]{:T(128)}) while((s32[]{:T(128)}, f32[8,512,128]{2,1,0:T(8,128)S(1)}, bf16[8,512,512]{2,1,0:T(8,128)(2,1)}, bf16[2048,512]{1,0:T(8,128)(2,1)}, ...), condition=%wide.region_2.3_spmd, body=%wide.region_1.2_spmd.sunk | while | flops 2688548864 | bytes 16515685 | solution.py:25
  114.9 3.1 fusion.48
  118.0 3.7 fusion.49
  121.7 3.1 fusion.48
  124.9 3.7 fusion.49
  128.6 3.1 fusion.48
  131.7 3.7 fusion.49
  135.4 3.1 fusion.48
  138.6 3.7 fusion.49
  142.3 3.1 fusion.48
  145.4 3.7 fusion.49
  149.1 3.1 fusion.48
  152.3 3.7 fusion.49
  156.0 3.1 fusion.48
  159.1 3.7 fusion.49
  162.8 3.1 fusion.48
  166.0 3.7 fusion.49
  169.7 1.3 copy-done.1
  171.0 60.5 %reduce-scatter.3.cloned.1.call-done = f32[256,128]{1,0:T(8,128)} async-done(((f32[4096,128]{1,0:T(8,128)}), f32[256,128]{1,0:T(8,128)}) %reduce-scatter.3.cloned.1.call-update) | async-done | bytes 131088 | tf_op jit(solution)/shard_map/reduce_scatter | solution.py:38
  232.5 68.0 %all-reduce.1 = (f32[128]{0:T(128)S(1)}, f32[128]{0:T(128)S(1)}) all-reduce(f32[128]{0:T(128)S(1)} %get-tuple-element.61, f32[128]{0:T(128)S(1)} %get-tuple-element.60), channel_id=1, replica_groups=mesh['row'=8,'col'=16] {'row','col'}, use_global_device_ids=true, to_apply=%region_7.8 | all-reduce | flops 256 | bytes 2048 | tf_op jit(solution)/shard_map/psum | solution.py:44
  302.7 1.1 fusion.28
  303.8 1.7 broadcast_divide_fusion
  305.8 41.2 %all-gather.8.cloned.1.call-done = f32[2048,128]{1,0:T(8,128)} async-done(((f32[256,128]{1,0:T(8,128)}), f32[2048,128]{1,0:T(8,128)}) %all-gather.8.cloned.1.call-update) | async-done | bytes 1048592 | tf_op jit(solution)/shard_map/all_gather | solution.py:37
  347.2 54.8 %while.21 = (s32[]{:T(128)}, f32[8,512,128]{2,1,0:T(8,128)S(1)}, bf16[8,512,512]{2,1,0:T(8,128)(2,1)}, bf16[2048,512]{1,0:T(8,128)(2,1)}, f32[2048,128]{1,0:T(8,128)}, /*index=5*/s32[]{:T(128)}) while((s32[]{:T(128)}, f32[8,512,128]{2,1,0:T(8,128)S(1)}, bf16[8,512,512]{2,1,0:T(8,128)(2,1)}, bf16[2048,512]{1,0:T(8,128)(2,1)}, ...), condition=%wide.region_12.13_spmd, body=%wide.region_11.12_spmd.sunk | while | flops 2688548864 | bytes 16515685 | solution.py:25
  347.2 3.1 fusion.53
  350.3 3.7 fusion.54
  354.1 3.1 fusion.53
  357.2 3.7 fusion.54
  360.9 3.1 fusion.53
  364.1 3.7 fusion.54
  367.8 3.1 fusion.53
  370.9 3.7 fusion.54
  374.6 3.1 fusion.53
  377.8 3.7 fusion.54
  381.5 3.1 fusion.53
  384.6 3.7 fusion.54
  388.3 3.1 fusion.53
  391.5 3.7 fusion.54
  395.2 3.1 fusion.53
  398.3 3.7 fusion.54
  402.0 1.3 copy-done
  403.4 62.6 %reduce-scatter.5.cloned.1.call-done = f32[256,128]{1,0:T(8,128)} async-done(((f32[4096,128]{1,0:T(8,128)}), f32[256,128]{1,0:T(8,128)}) %reduce-scatter.5.cloned.1.call-update) | async-done | bytes 131088 | tf_op jit(solution)/shard_map/reduce_scatter | solution.py:38
  467.1 67.5 %all-reduce = (f32[128]{0:T(128)S(1)}, f32[128]{0:T(128)S(1)}) all-reduce(f32[128]{0:T(128)S(1)} %get-tuple-element.59, f32[128]{0:T(128)S(1)} %get-tuple-element.58), channel_id=1, replica_groups=mesh['row'=8,'col'=16] {'row','col'}, use_global_device_ids=true, to_apply=%region_17.18 | all-reduce | flops 256 | bytes 2048 | tf_op jit(solution)/shard_map/psum | solution.py:44
  536.7 1.1 fusion.27
  (66 shorter events, 9.0 us)
Async XLA Ops:
  7.2 51.8 %all-gather.6.cloned.1.call-start = ((), (), s32[]{:S(2)}) async-start(), calls=%async_computation.3 | async-start | bytes 1179648 | tf_op jit(solution)/shard_map/all_gather | solution.py:37
  9.9 104.8 %all-gather.4.cloned.1.call-start = ((), (), s32[]{:S(2)}) async-start(), calls=%async_computation.2 | async-start | bytes 2359296 | tf_op jit(solution)/shard_map/all_gather | solution.py:32
  11.7 219.8 %reduce-scatter.3.cloned.1.call-start = ((), (), s32[]{:S(2)}) async-start(), calls=%async_computation.4 | async-start | bytes 2228224 | tf_op jit(solution)/shard_map/reduce_scatter | solution.py:38
  114.8 116.7 %copy-start.3 = (f32[256,128]{1,0:T(8,128)S(1)}, f32[256,128]{1,0:T(8,128)}, u32[]{:S(2)}) copy-start(f32[256,128]{1,0:T(8,128)} %param.7) | copy-start | bytes 393220
  114.8 3.1 copy-start.5
  121.7 3.1 copy-start.5
  128.6 3.1 copy-start.5
  135.4 3.1 copy-start.5
  142.3 3.1 copy-start.5
  149.1 3.1 copy-start.5
  156.0 3.1 copy-start.5
  162.8 3.1 copy-start.5
  169.7 1.3 copy-start.1
  171.0 176.0 %all-gather.8.cloned.1.call-start = ((), (), s32[]{:S(2)}) async-start(), calls=%async_computation.5 | async-start | bytes 1179648 | tf_op jit(solution)/shard_map/all_gather | solution.py:37
  305.6 160.4 %reduce-scatter.5.cloned.1.call-start = ((), (), s32[]{:S(2)}) async-start(), calls=%async_computation.6 | async-start | bytes 2228224 | tf_op jit(solution)/shard_map/reduce_scatter | solution.py:38
  347.2 118.8 %copy-start.2 = (f32[256,128]{1,0:T(8,128)S(1)}, f32[256,128]{1,0:T(8,128)}, u32[]{:S(2)}) copy-start(f32[256,128]{1,0:T(8,128)} %reduce-scatter.3.cloned.1.call-done) | copy-start | bytes 393220
  347.2 3.1 copy-start.6
  354.1 3.1 copy-start.6
  360.9 3.1 copy-start.6
  367.8 3.1 copy-start.6
  374.6 3.1 copy-start.6
  381.5 3.1 copy-start.6
  388.3 3.1 copy-start.6
  395.2 3.1 copy-start.6
  402.0 1.4 copy-start
  537.9 0.8 copy-start.4
Sparse Core Ops, SparseCore 0:
  10.9 48.0 all-gather.5
  61.3 53.3 all-gather.3
  171.1 60.3 reduce-scatter.2
  305.7 41.2 all-gather.7
  403.5 62.4 reduce-scatter.4
where the time goes:
time: 546 us; the launch traced here: 545 us
  waiting for transfers between devices  267 us (49%)
  blocking collectives  136 us (25%)
  matrix products  109 us (20%)
  between operations  13.9 us (3%)
  other arithmetic  13.8 us (3%)
    psum x2, blocking collectives, on_device(): lax.psum((jnp.sum(members, axis=0), jnp.sum(members * scores, axis=0)), (...  136 us
    reduce_scatter x2, waiting for transfers between devices, on_device(): lax.psum_scatter(kernel_product(features, column_panel, members_column),...  123 us
    all_gather x2, waiting for transfers between devices, on_device(): members_column = lax.all_gather(members, 'row', axis=0, tiled=True)  88.4 us
    dot_general x16, matrix products, block_product(): jnp.dot(kernel, members, precision=lax.Precision.HIGHEST, preferred_eleme...  59 us
    all_gather x1, waiting for transfers between devices, on_device(): column_panel = lax.all_gather(own_rows, 'row', axis=0, tiled=True)  55.7 us
    dot_general x16, matrix products, block_product(): jnp.einsum('bf,nf->bn', block, right_rows, preferred_element_type=jnp.flo...  50 us
  transfers between devices with their start and end apart: 5, of which 5 were waited for; matrix products, arithmetic and copies ran while one was open for 0% of the time, Pallas kernels for 0%

commit v1 on v0

v1 whole, which is shorter than its diff:
```python
import functools

import jax
import jax.numpy as jnp
from jax import lax
from jax.experimental import pallas as pl
from jax.experimental.pallas import tpu as pltpu
from jax.sharding import PartitionSpec as P

ITERS = 2
SUB = 256
MESH = pl.DeviceIdType.MESH
BF16 = jnp.bfloat16
F32 = jnp.float32


def rows(start, size=SUB):
    return pl.ds(start if isinstance(start, int) else pl.multiple_of(start, 128), size)


def softmax_rows(raised):
    return raised / jnp.sum(raised, axis=1, keepdims=True)


def kernel(
    feat, logits, memb_out, std_out,
    frow, fcol, mem0, mem1, p_hi, p_lo, own, total,
    mid, near, side, vec,
    load_sem, f_send, f_recv, m_send, m_recv, r_send, r_recv, v_send, v_recv,
):
    clusters = logits.shape[1]
    width = feat.shape[1]
    row, col = lax.axis_index("row"), lax.axis_index("col")
    z, xh = row // 2, row % 2
    y, xl, core = col // 4, (col // 2) % 2, col % 2

    def device(dz=0, dx1=0, dy=0, dx2=0, dk=0):
        new_xh = (xh + dx1) % 2
        new_xl = (xl + dx1 + dx2) % 2
        return (
            ((z + dz) % 4) * 2 + new_xh,
            ((y + dy) % 4) * 4 + new_xl * 2 + (core + dk) % 2,
        )

    z_up, z_down = device(dz=1), device(dz=3)
    cross, partner = device(dx1=1), device(dk=1)
    y_up, y_down, across = device(dy=1), device(dy=3), device(dx2=1)
    reduce_group = [(dy, dx) for dy in range(4) for dx in range(2)][1:]
    gather_group = [(dz, dx, dk) for dz in range(4) for dx in range(2) for dk in range(2)][1:]

    barrier = pltpu.get_barrier_semaphore()
    for dy, dx in reduce_group:
        pl.semaphore_signal(barrier, inc=1, device_id=device(dy=dy, dx2=dx), device_id_type=MESH)
    for dz, dx, dk in gather_group:
        pl.semaphore_signal(
            barrier, inc=1, device_id=device(dz=dz, dx1=dx, dk=dk), device_id_type=MESH
        )

    order = [(2, 1), (2, 0), (1, 1), (3, 1), (1, 0), (3, 0), (0, 1), (0, 0)]
    loads = []
    for u, (dy, dx) in enumerate(order):
        block = ((y + dy) % 4) * 4 + ((xl + dx) % 2) * 2 + core
        loads.append(
            pltpu.make_async_copy(
                feat.at[rows(block * SUB)], frow.at[rows(u * SUB)], load_sem.at[u]
            )
        )
    loads.append(
        pltpu.make_async_copy(
            feat.at[rows((y * 4 + xl * 2) * SUB, 2 * SUB)], fcol.at[rows(0, 2 * SUB)], load_sem.at[8]
        )
    )
    for load in loads:
        load.start()

    def put_members(members, mem):
        hi = members.astype(BF16)
        lo = (members - hi.astype(F32)).astype(BF16)
        own[...] = members
        mem[rows(core * SUB), 0:clusters] = hi
        mem[rows(core * SUB), clusters : 2 * clusters] = lo

    put_members(softmax_rows(jnp.exp(logits[...])), mem0)
    pl.semaphore_wait(barrier, len(reduce_group) + len(gather_group))

    class Stream:
        def __init__(self, buf, send, recv, own_src=None):
            self.buf, self.send, self.recv = buf, send, recv
            self.own_src = own_src
            self.sent = 0
            self.started = []

        def at(self, slot, half=None, other=False):
            part = 1 - core if other else core
            start = slot * 2 * SUB + part * SUB
            if half is None:
                return self.buf.at[rows(start)]
            return self.buf.at[rows(start + half * (SUB // 2), SUB // 2)]

        def make(self, src, dst, where, sem):
            n = self.sent
            self.sent += 1
            self.started.append((n, src))
            return pltpu.make_async_remote_copy(
                src_ref=src(), dst_ref=dst, send_sem=self.send.at[n], recv_sem=self.recv.at[sem],
                device_id=where, device_id_type=MESH,
            )

        def wait(self, *sems):
            for s in sems:
                if s >= 9:
                    dst = self.at(s - 9, other=True)
                elif s >= 8:
                    dst = self.at(7)
                elif s >= 6:
                    dst = self.at(6, s - 6)
                else:
                    dst = self.at(s)
                pltpu.make_async_copy(dst, dst, self.recv.at[s]).wait()

        def send_own(self):
            src = self.own_src or (lambda: self.at(0))
            self.make(src, self.at(2), z_up, 2).start()
            self.make(src, self.at(3), z_down, 3).start()
            self.make(src, self.at(1), cross, 1).start()
            if self.own_src is None:
                self.make(src, self.at(0), partner, 9).start()

        def to_partner(self, slot):
            self.make(lambda: self.at(slot), self.at(slot), partner, 9 + slot).start()

        def forward_1(self):
            self.wait(1)
            self.make(lambda: self.at(1), self.at(4), z_up, 4).start()
            self.make(lambda: self.at(1), self.at(5), z_down, 5).start()
            self.to_partner(1)

        def forward_2(self):
            self.wait(2)
            self.make(lambda: self.at(2, 0), self.at(6, 0), z_up, 6).start()
            self.to_partner(2)

        def forward_3(self):
            self.wait(3)
            self.make(lambda: self.at(3, 1), self.at(6, 1), z_down, 7).start()
            self.to_partner(3)

        def forward_45(self):
            self.wait(4)
            self.to_partner(4)
            self.wait(5)
            self.to_partner(5)

        def forward_6(self):
            self.wait(6, 7)
            self.make(lambda: self.at(6), self.at(7), cross, 8).start()
            self.to_partner(6)

        def forward_7(self):
            self.wait(8)
            self.to_partner(7)

        def finish(self):
            for n, src in self.started:
                pltpu.make_async_copy(src(), src(), self.send.at[n]).wait()

    feats = Stream(fcol, f_send, f_recv, lambda: feat.at[rows(col * SUB)])
    mems = [
        Stream(mem, m_send.at[i], m_recv.at[i]) for i, mem in enumerate((mem0, mem1))
    ]
    feats.send_own()
    mems[0].send_own()

    for load in loads:
        load.wait()

    def scale(i, carry):
        frow[rows(i * SUB), :] = frow[rows(i * SUB), :] * (1.0 / width)
        return carry

    lax.fori_loop(0, 8, scale, 0)

    def inner(first, last):
        def block(b, carry):
            at = rows(b * SUB)
            x = lax.dot_general(
                frow[...], fcol[at, :], (((1,), (1,)), ((), ())), preferred_element_type=F32
            )
            p = x * (3.0 + x * (3.0 + x))
            hi = p.astype(BF16)
            p_hi[:, at] = hi
            p_lo[:, at] = (p - hi.astype(F32)).astype(BF16)
            return carry

        lax.fori_loop(2 * first, 2 * last, block, 0)

    def product(at, cols, mem):
        both = jnp.dot(p_hi[at, cols], mem[cols, :], preferred_element_type=F32)
        low = jnp.dot(p_lo[at, cols], mem[cols, 0:clusters], preferred_element_type=F32)
        return both[:, :clusters] + both[:, clusters:] + low

    def first_pass(mem, actions):
        def chunk(i, carry):
            at = rows(i * 512, 512)
            total[at, :] = product(at, slice(0, 2048), mem)
            for step, action in actions:
                pl.when(i == step)(action)
            return carry

        lax.fori_loop(0, 4, chunk, 0)

    def exchange(members, buf, send, recv, group):
        buf[0] = jnp.broadcast_to(members, buf.shape[1:])
        copies = []
        for j, (where, slot) in enumerate(group):
            copies.append(
                pltpu.make_async_remote_copy(
                    src_ref=buf.at[0], dst_ref=buf.at[slot], send_sem=send.at[j],
                    recv_sem=recv.at[slot], device_id=where, device_id_type=MESH,
                )
            )
            copies[-1].start()

        def finish():
            for copy in copies:
                copy.wait_send()
            for _, slot in group:
                pltpu.make_async_copy(buf.at[slot], buf.at[slot], recv.at[slot]).wait()
            out = buf[0, 0:1, :]
            for _, slot in group:
                out = out + buf[slot, 0:1, :]
            return out

        return finish

    near_ids = [(device(dy=dy, dx2=dx), ((4 - dy) % 4) * 2 + dx) for dy, dx in reduce_group]
    far_ids = [
        (device(dz=dz, dx1=dx, dk=dk), ((4 - dz) % 4) * 4 + dx * 2 + dk) for dz, dx, dk in gather_group
    ]

    feats.forward_1()
    feats.forward_2()
    feats.forward_3()
    inner(0, 1)
    mems[0].forward_1()
    mems[0].forward_2()
    mems[0].forward_3()
    feats.wait(10, 11, 12)
    inner(1, 4)

    for it in range(ITERS):
        mem, stream = (mem0, mem1)[it], mems[it]
        if it == 0:
            feats.forward_45()
            feats.forward_6()
            stream.wait(9, 10, 11, 12)
            first_pass(
                mem,
                [(0, stream.forward_45), (1, feats.forward_7), (2, stream.forward_6), (3, stream.forward_7)],
            )
            feats.wait(13, 14)
            inner(4, 6)
            feats.wait(15, 16)
            inner(6, 8)
        else:
            stream.send_own()
            stream.forward_1()
            stream.forward_2()
            stream.forward_3()
            stream.wait(9, 10, 11, 12)
            first_pass(
                mem, [(1, stream.forward_45), (2, stream.forward_6), (3, stream.forward_7)]
            )
        stream.wait(13, 14, 15, 16)

        ones = jnp.ones((16, 8 * 2 * SUB), BF16)
        panel = jnp.dot(ones, mem[...], preferred_element_type=F32)[0:1]
        size_done = exchange(
            panel[:, :clusters] + panel[:, clusters:], vec.at[it, pl.ds(0, 8)],
            v_send.at[it, 0], v_recv.at[it, 0], near_ids,
        )

        rs = functools.partial(
            pltpu.make_async_remote_copy, device_id_type=MESH
        )
        sends = {}
        for j, dx in enumerate((1, 0)):
            u = j
            sends[u] = [
                rs(total.at[rows(u * SUB, 128)], mid.at[it, j, 0], r_send.at[it, 2 * j], r_recv.at[it, 2 * j], device_id=y_up),
                rs(total.at[rows(u * SUB + 128, 128)], mid.at[it, j, 1], r_send.at[it, 2 * j + 1], r_recv.at[it, 2 * j + 1], device_id=y_down),
            ]
            up, down = 2 + 2 * j, 3 + 2 * j
            sends[up] = [rs(total.at[rows(up * SUB)], near.at[it, j, 0], r_send.at[it, 4 + 2 * j], r_recv.at[it, 4 + 2 * j], device_id=y_up)]
            sends[down] = [rs(total.at[rows(down * SUB)], near.at[it, j, 1], r_send.at[it, 5 + 2 * j], r_recv.at[it, 5 + 2 * j], device_id=y_down)]
        sends[6] = [rs(total.at[rows(6 * SUB)], side.at[it], r_send.at[it, 8], r_recv.at[it, 8], device_id=across)]

        def ready(ref, n):
            pltpu.make_async_copy(ref, ref, r_recv.at[it, n]).wait()

        def after(u):
            def action():
                if 2 <= u <= 5:
                    j, half = (u - 2) // 2, u % 2
                    ready(mid.at[it, j, half], 2 * j + half)
                    at = rows(u * SUB + 128 * half, 128)
                    total[at, :] = total[at, :] + mid[it, j, half]
                if u >= 6:
                    j = u - 6
                    ready(near.at[it, j, 0], 4 + 2 * j)
                    ready(near.at[it, j, 1], 5 + 2 * j)
                    at = rows(u * SUB)
                    total[at, :] = total[at, :] + near[it, j, 0] + near[it, j, 1]
                for copy in sends.get(u, []):
                    copy.start()

            return action

        def step(u, carry):
            at = rows(u * SUB)
            total[at, :] = total[at, :] + product(at, slice(2048, 4096), mem)
            for v in range(8):
                pl.when(u == v)(after(v))
            return carry

        lax.fori_loop(0, 8, step, 0)
        size = size_done()
        ready(side.at[it], 8)
        for copies in sends.values():
            for copy in copies:
                copy.wait_send()
        scores = total[rows(7 * SUB), :] + side[it]
        members = own[...]
        weighted = exchange(
            jnp.sum(members * scores, axis=0, keepdims=True), vec.at[it, pl.ds(8, 8)],
            v_send.at[it, 1], v_recv.at[it, 1], near_ids,
        )()
        weighted = exchange(
            weighted, vec.at[it, pl.ds(16, 16)], v_send.at[it, 2], v_recv.at[it, 2], far_ids,
        )()
        distance = weighted / (size * size) - 2.0 * scores / size
        centered = distance - jnp.mean(distance, axis=1, keepdims=True)
        spread = jnp.mean(centered * centered, axis=1, keepdims=True)
        standardized = centered / jnp.sqrt(spread + 1e-06)
        members = softmax_rows(jnp.exp(-2.0 * standardized))
        if it + 1 < ITERS:
            put_members(members, mem1)
        else:
            memb_out[...] = members
            std_out[...] = standardized
        stream.finish()
    feats.finish()


def on_device(features, logits):
    frames, clusters = logits.shape
    width = features.shape[1]
    tall, wide = 8 * SUB, 16 * SUB
    vmem = pl.BlockSpec(memory_space=pltpu.VMEM)
    out = jax.ShapeDtypeStruct((frames, clusters), F32)
    dma = pltpu.SemaphoreType.DMA
    return pl.pallas_call(
        kernel,
        out_shape=(out, out),
        in_specs=[pl.BlockSpec(memory_space=pl.ANY), vmem],
        out_specs=(vmem, vmem),
        scratch_shapes=[
            pltpu.VMEM((tall, width), BF16),
            pltpu.VMEM((wide, width), BF16),
            pltpu.VMEM((wide, 2 * clusters), BF16),
            pltpu.VMEM((wide, 2 * clusters), BF16),
            pltpu.VMEM((tall, wide), BF16),
            pltpu.VMEM((tall, wide), BF16),
            pltpu.VMEM((SUB, clusters), F32),
            pltpu.VMEM((tall, clusters), F32),
            pltpu.VMEM((ITERS, 2, 2, 128, clusters), F32),
            pltpu.VMEM((ITERS, 2, 2, SUB, clusters), F32),
            pltpu.VMEM((ITERS, SUB, clusters), F32),
            pltpu.VMEM((ITERS, 32, 8, clusters), F32),
            dma((9,)),
            dma((24,)),
            dma((17,)),
            dma((ITERS, 24)),
            dma((ITERS, 17)),
            dma((ITERS, 9)),
            dma((ITERS, 9)),
            dma((ITERS, 3, 16)),
            dma((ITERS, 3, 16)),
        ],
        compiler_params=pltpu.CompilerParams(
            collective_id=0, has_side_effects=True, vmem_limit_bytes=62 * 1024 * 1024
        ),
    )(features, logits)


def solution(mesh):
    return jax.shard_map(
        on_device,
        mesh=mesh,
        in_specs=(P("row", None), P(("row", "col"), None)),
        out_specs=(P(("row", "col"), None), P(("row", "col"), None)),
        check_vma=False,
    )
```

time: 546 us -> 121 us (0.22)
  waiting for transfers between devices: 267 us -> 0 us
  blocking collectives: 136 us -> 0 us
  Pallas kernels: 0 us -> 117 us
  matrix products: 109 us -> 0 us
  other arithmetic: 13.8 us -> 0 us
  between operations: 13.9 us -> 0.64 us
    all_gather x3 -> x0, waiting for transfers between devices: 144 us -> none  [the longest x2 88.4 us: on_device(): members_column = lax.all_gather(members, 'row', axis=0, tiled=True)]
    psum x2 -> x0, blocking collectives: 136 us -> none  [on_device(): lax.psum((jnp.sum(members, axis=0), jnp.sum(members * scores, axis=0)), (...]
    reduce_scatter x2 -> x0, waiting for transfers between devices: 123 us -> none  [on_device(): lax.psum_scatter(kernel_product(features, column_panel, members_column),...]
    pallas_call x0 -> x1, Pallas kernels: none -> 117 us  [on_device(): pl.pallas_call(kernel, out_shape=(out, out), in_specs=[pl.BlockSpec(memor...]
    dot_general x32 -> x0, matrix products: 109 us -> none  [the longest x16 59 us: block_product(): jnp.dot(kernel, members, precision=lax.Precision.HIGHEST, preferred_eleme...]
    reduce_sum x9 -> x0, other arithmetic: 9.61 us -> none  [the longest x3 3.29 us: on_device(): members = raised / jnp.sum(raised, axis=1, keepdims=True)]
  transfers between devices with their start and end apart: 5 -> 0, of which waited for: 5 -> 0; matrix products, arithmetic and copies ran while one was open for 0% -> 0% of each run, Pallas kernels for 0% -> 0%
where the time goes in v1:
time: 121 us
  Pallas kernels  117 us (97%)
  local copies, waits for them, and re-layouts  3.14 us (3%)
    pallas_call x1, Pallas kernels, on_device(): pl.pallas_call(kernel, out_shape=(out, out), in_specs=[pl.BlockSpec(memor...  117 us
    unnamed x2, local copies, waits for them, and re-layouts  3.14 us

profile of v1, /device:TPU:1, one launch (start us, length us, event | category | flops | bytes accessed | tf_op | source)
XLA Modules:
  0.0 120.9 jit_solution(15783707363717966381)
XLA Ops:
  0.6 117.1 %shard_map.41 = (f32[256,128]{1,0:T(8,128)}, f32[256,128]{1,0:T(8,128)}) custom-call(bf16[4096,512]{1,0:T(8,128)(2,1)} %feat.1, f32[256,128]{1,0:T(8,128)} %logits.1), custom_call_target="tpu_custom_call" | custom-call | tf_op jit(solution)/shard_map/pallas_call | solution.py:362
  117.7 1.6 %copy.6 = f32[256,128]{1,0:T(8,128)} copy(f32[256,128]{1,0:T(8,128)} %get-tuple-element.4) | data formatting | bytes 262144
  119.3 1.6 %copy.7 = f32[256,128]{1,0:T(8,128)} copy(f32[256,128]{1,0:T(8,128)} %get-tuple-element.5) | data formatting | bytes 262144

commit v2 on v1

--- a/solution.py
+++ b/solution.py
@@ -1,5 +1,3 @@
-import functools
-
 import jax
 import jax.numpy as jnp
 from jax import lax
@@ -24,9 +22,9 @@
 
 def kernel(
     feat, logits, memb_out, std_out,
-    frow, fcol, mem0, mem1, p_hi, p_lo, own, total,
-    mid, near, side, vec,
-    load_sem, f_send, f_recv, m_send, m_recv, r_send, r_recv, v_send, v_recv,
+    frow, fcol, mem0, mem1, rows0, rows1, p_hi, p_lo, total, wsum,
+    inbox, vec,
+    load_sem, f_send, f_recv, m_send, m_recv, a_send, a_recv, r_send, r_recv, v_send, v_recv,
 ):
     clusters = logits.shape[1]
     width = feat.shape[1]
@@ -42,19 +40,16 @@
             ((y + dy) % 4) * 4 + new_xl * 2 + (core + dk) % 2,
         )
 
-    z_up, z_down = device(dz=1), device(dz=3)
+    z_up, z_down, z_far = device(dz=1), device(dz=3), device(dz=2)
     cross, partner = device(dx1=1), device(dk=1)
-    y_up, y_down, across = device(dy=1), device(dy=3), device(dx2=1)
+    y_up, y_down, y_far, across = device(dy=1), device(dy=3), device(dy=2), device(dx2=1)
     reduce_group = [(dy, dx) for dy in range(4) for dx in range(2)][1:]
     gather_group = [(dz, dx, dk) for dz in range(4) for dx in range(2) for dk in range(2)][1:]
 
     barrier = pltpu.get_barrier_semaphore()
-    for dy, dx in reduce_group:
-        pl.semaphore_signal(barrier, inc=1, device_id=device(dy=dy, dx2=dx), device_id_type=MESH)
-    for dz, dx, dk in gather_group:
-        pl.semaphore_signal(
-            barrier, inc=1, device_id=device(dz=dz, dx1=dx, dk=dk), device_id_type=MESH
-        )
+    nearest = (z_up, z_down, cross, partner, y_up, y_down, across)
+    for where in nearest:
+        pl.semaphore_signal(barrier, inc=1, device_id=where, device_id_type=MESH)
 
     order = [(2, 1), (2, 0), (1, 1), (3, 1), (1, 0), (3, 0), (0, 1), (0, 0)]
     loads = []
@@ -73,15 +68,15 @@
     for load in loads:
         load.start()
 
-    def put_members(members, mem):
+    def put_members(members, mem, tile_rows):
         hi = members.astype(BF16)
         lo = (members - hi.astype(F32)).astype(BF16)
-        own[...] = members
-        mem[rows(core * SUB), 0:clusters] = hi
-        mem[rows(core * SUB), clusters : 2 * clusters] = lo
-
-    put_members(softmax_rows(jnp.exp(logits[...])), mem0)
-    pl.semaphore_wait(barrier, len(reduce_group) + len(gather_group))
+        for ref, start in ((mem, core * SUB), (tile_rows, 7 * SUB)):
+            ref[rows(start), 0:clusters] = hi
+            ref[rows(start), clusters : 2 * clusters] = lo
+
+    put_members(softmax_rows(jnp.exp(logits[...])), mem0, rows0)
+    pl.semaphore_wait(barrier, len(nearest))
 
     class Stream:
         def __init__(self, buf, send, recv, own_src=None):
@@ -112,7 +107,7 @@
                     dst = self.at(s - 9, other=True)
                 elif s >= 8:
                     dst = self.at(7)
-                elif s >= 6:
+                elif s >= 6 and self.own_src is not None:
                     dst = self.at(6, s - 6)
                 else:
                     dst = self.at(s)
@@ -135,14 +130,19 @@
             self.make(lambda: self.at(1), self.at(5), z_down, 5).start()
             self.to_partner(1)
 
+        def send_far(self):
+            self.make(lambda: self.at(0), self.at(6), z_far, 6).start()
+
         def forward_2(self):
             self.wait(2)
-            self.make(lambda: self.at(2, 0), self.at(6, 0), z_up, 6).start()
+            if self.own_src is not None:
+                self.make(lambda: self.at(2, 0), self.at(6, 0), z_up, 6).start()
             self.to_partner(2)
 
         def forward_3(self):
             self.wait(3)
-            self.make(lambda: self.at(3, 1), self.at(6, 1), z_down, 7).start()
+            if self.own_src is not None:
+                self.make(lambda: self.at(3, 1), self.at(6, 1), z_down, 7).start()
             self.to_partner(3)
 
         def forward_45(self):
@@ -152,7 +152,9 @@
             self.to_partner(5)
 
         def forward_6(self):
-            self.wait(6, 7)
+            self.wait(6)
+            if self.own_src is not None:
+                self.wait(7)
             self.make(lambda: self.at(6), self.at(7), cross, 8).start()
             self.to_partner(6)
 
@@ -165,11 +167,30 @@
                 pltpu.make_async_copy(src(), src(), self.send.at[n]).wait()
 
     feats = Stream(fcol, f_send, f_recv, lambda: feat.at[rows(col * SUB)])
-    mems = [
-        Stream(mem, m_send.at[i], m_recv.at[i]) for i, mem in enumerate((mem0, mem1))
-    ]
+    mems = [Stream(mem, m_send.at[i], m_recv.at[i]) for i, mem in enumerate((mem0, mem1))]
+
+    def row_copy(it, dy, dx):
+        there = order.index(((4 - dy) % 4, dx))
+        buf = (rows0, rows1)[it]
+        return pltpu.make_async_remote_copy(
+            src_ref=buf.at[rows(7 * SUB)], dst_ref=buf.at[rows(there * SUB)],
+            send_sem=a_send.at[it, there], recv_sem=a_recv.at[it, there],
+            device_id=device(dy=dy, dx2=dx), device_id_type=MESH,
+        )
+
+    def send_rows(it, group):
+        for dy, dx in group:
+            row_copy(it, dy, dx).start()
+
+    def wait_rows(it, group):
+        for dy, dx in group:
+            row_copy(it, (4 - dy) % 4, dx).wait_recv()
+
+    row_near, row_mid, row_far = [(1, 0), (3, 0), (0, 1)], [(2, 0), (1, 1), (3, 1)], [(2, 1)]
+
     feats.send_own()
     mems[0].send_own()
+    send_rows(0, row_near)
 
     for load in loads:
         load.wait()
@@ -199,10 +220,11 @@
         low = jnp.dot(p_lo[at, cols], mem[cols, 0:clusters], preferred_element_type=F32)
         return both[:, :clusters] + both[:, clusters:] + low
 
-    def first_pass(mem, actions):
+    def column_pass(mem, first, last, actions=()):
         def chunk(i, carry):
             at = rows(i * 512, 512)
-            total[at, :] = product(at, slice(0, 2048), mem)
+            part = product(at, slice(first * 2 * SUB, last * 2 * SUB), mem)
+            total[at, :] = part if first == 0 else total[at, :] + part
             for step, action in actions:
                 pl.when(i == step)(action)
             return carry
@@ -238,40 +260,56 @@
         (device(dz=dz, dx1=dx, dk=dk), ((4 - dz) % 4) * 4 + dx * 2 + dk) for dz, dx, dk in gather_group
     ]
 
-    feats.forward_1()
-    feats.forward_2()
-    feats.forward_3()
-    inner(0, 1)
-    mems[0].forward_1()
-    mems[0].forward_2()
-    mems[0].forward_3()
-    feats.wait(10, 11, 12)
-    inner(1, 4)
-
     for it in range(ITERS):
-        mem, stream = (mem0, mem1)[it], mems[it]
+        mem, stream, tile_rows = (mem0, mem1)[it], mems[it], (rows0, rows1)[it]
         if it == 0:
-            feats.forward_45()
+            inner(0, 1)
+            stream.wait(9)
+            column_pass(mem, 0, 1)
+            feats.forward_2()
+            feats.forward_3()
+            feats.forward_1()
+            wait_rows(0, row_near)
+            send_rows(0, row_mid)
+            stream.send_far()
+            stream.forward_1()
+            feats.wait(10, 11, 12)
+            inner(1, 2)
+            stream.forward_2()
+            stream.forward_3()
+            wait_rows(0, row_mid)
+            send_rows(0, row_far)
+            inner(2, 3)
             feats.forward_6()
-            stream.wait(9, 10, 11, 12)
-            first_pass(
-                mem,
-                [(0, stream.forward_45), (1, feats.forward_7), (2, stream.forward_6), (3, stream.forward_7)],
+            inner(3, 4)
+            stream.wait(10, 11, 12)
+            column_pass(
+                mem, 1, 4,
+                [(0, feats.forward_45), (1, stream.forward_6), (2, stream.forward_45)],
             )
             feats.wait(13, 14)
-            inner(4, 6)
+            inner(4, 5)
+            feats.forward_7()
+            inner(5, 6)
+            stream.forward_7()
             feats.wait(15, 16)
             inner(6, 8)
+            wait_rows(0, row_far)
         else:
             stream.send_own()
+            stream.send_far()
+            send_rows(it, row_near + row_mid + row_far)
+            stream.wait(9)
+            column_pass(mem, 0, 1)
             stream.forward_1()
             stream.forward_2()
             stream.forward_3()
-            stream.wait(9, 10, 11, 12)
-            first_pass(
-                mem, [(1, stream.forward_45), (2, stream.forward_6), (3, stream.forward_7)]
-            )
-        stream.wait(13, 14, 15, 16)
+            stream.wait(10, 11, 12)
+            column_pass(mem, 1, 4, [(2, stream.forward_6), (3, stream.forward_45)])
+            wait_rows(it, row_near + row_mid + row_far)
+        stream.wait(13, 14)
+        column_pass(mem, 4, 6, [(3, stream.forward_7)] if it else ())
+        stream.wait(15, 16)
 
         ones = jnp.ones((16, 8 * 2 * SUB), BF16)
         panel = jnp.dot(ones, mem[...], preferred_element_type=F32)[0:1]
@@ -280,75 +318,66 @@
             v_send.at[it, 0], v_recv.at[it, 0], near_ids,
         )
 
-        rs = functools.partial(
-            pltpu.make_async_remote_copy, device_id_type=MESH
-        )
-        sends = {}
-        for j, dx in enumerate((1, 0)):
-            u = j
-            sends[u] = [
-                rs(total.at[rows(u * SUB, 128)], mid.at[it, j, 0], r_send.at[it, 2 * j], r_recv.at[it, 2 * j], device_id=y_up),
-                rs(total.at[rows(u * SUB + 128, 128)], mid.at[it, j, 1], r_send.at[it, 2 * j + 1], r_recv.at[it, 2 * j + 1], device_id=y_down),
-            ]
-            up, down = 2 + 2 * j, 3 + 2 * j
-            sends[up] = [rs(total.at[rows(up * SUB)], near.at[it, j, 0], r_send.at[it, 4 + 2 * j], r_recv.at[it, 4 + 2 * j], device_id=y_up)]
-            sends[down] = [rs(total.at[rows(down * SUB)], near.at[it, j, 1], r_send.at[it, 5 + 2 * j], r_recv.at[it, 5 + 2 * j], device_id=y_down)]
-        sends[6] = [rs(total.at[rows(6 * SUB)], side.at[it], r_send.at[it, 8], r_recv.at[it, 8], device_id=across)]
-
-        def ready(ref, n):
-            pltpu.make_async_copy(ref, ref, r_recv.at[it, n]).wait()
-
-        def after(u):
-            def action():
-                if 2 <= u <= 5:
-                    j, half = (u - 2) // 2, u % 2
-                    ready(mid.at[it, j, half], 2 * j + half)
-                    at = rows(u * SUB + 128 * half, 128)
-                    total[at, :] = total[at, :] + mid[it, j, half]
-                if u >= 6:
-                    j = u - 6
-                    ready(near.at[it, j, 0], 4 + 2 * j)
-                    ready(near.at[it, j, 1], 5 + 2 * j)
-                    at = rows(u * SUB)
-                    total[at, :] = total[at, :] + near[it, j, 0] + near[it, j, 1]
-                for copy in sends.get(u, []):
-                    copy.start()
-
-            return action
+        def score_copy(u, slot, where):
+            return pltpu.make_async_remote_copy(
+                src_ref=total.at[rows(u * SUB)], dst_ref=inbox.at[it, slot],
+                send_sem=r_send.at[it, slot], recv_sem=r_recv.at[it, slot],
+                device_id=where, device_id_type=MESH,
+            )
+
+        routes = [
+            (0, 0, across), (2, 1, y_up), (3, 2, y_down), (4, 3, y_up), (5, 4, y_down), (1, 5, y_far), (6, 6, across),
+        ]
+        wsum[...] = jnp.zeros_like(wsum)
 
         def step(u, carry):
             at = rows(u * SUB)
-            total[at, :] = total[at, :] + product(at, slice(2048, 4096), mem)
-            for v in range(8):
-                pl.when(u == v)(after(v))
+            part = total[at, :] + product(at, slice(6 * 2 * SUB, 8 * 2 * SUB), mem)
+            total[at, :] = part
+            weights = tile_rows[at, 0:clusters].astype(F32) + tile_rows[at, clusters : 2 * clusters].astype(F32)
+            wsum[...] += jnp.sum((weights * part).reshape(SUB // 8, 8, clusters), axis=0)
+            for v, slot, where in routes[:5]:
+                pl.when(u == v)(lambda v=v, slot=slot, where=where: score_copy(v, slot, where).start())
             return carry
 
         lax.fori_loop(0, 8, step, 0)
+        weighted_done = exchange(
+            jnp.sum(wsum[...], axis=0, keepdims=True), vec.at[it, pl.ds(8, 8)],
+            v_send.at[it, 1], v_recv.at[it, 1], near_ids,
+        )
+        score_copy(*routes[0]).wait_recv()
+        total[rows(SUB), :] = total[rows(SUB), :] + inbox[it, 0]
+        score_copy(*routes[5]).start()
+        score_copy(*routes[1]).wait_recv()
+        score_copy(*routes[2]).wait_recv()
+        total[rows(6 * SUB), :] = total[rows(6 * SUB), :] + inbox[it, 1] + inbox[it, 2]
+        score_copy(*routes[6]).start()
+        weighted_done = exchange(
+            weighted_done(), vec.at[it, pl.ds(16, 16)], v_send.at[it, 2], v_recv.at[it, 2], far_ids,
+        )
         size = size_done()
-        ready(side.at[it], 8)
-        for copies in sends.values():
-            for copy in copies:
-                copy.wait_send()
-        scores = total[rows(7 * SUB), :] + side[it]
-        members = own[...]
-        weighted = exchange(
-            jnp.sum(members * scores, axis=0, keepdims=True), vec.at[it, pl.ds(8, 8)],
-            v_send.at[it, 1], v_recv.at[it, 1], near_ids,
-        )()
-        weighted = exchange(
-            weighted, vec.at[it, pl.ds(16, 16)], v_send.at[it, 2], v_recv.at[it, 2], far_ids,
-        )()
+        weighted = weighted_done()
+        for route in routes[3:]:
+            score_copy(*route).wait_recv()
+        scores = total[rows(7 * SUB), :]
+        for slot in range(3, 7):
+            scores = scores + inbox[it, slot]
         distance = weighted / (size * size) - 2.0 * scores / size
         centered = distance - jnp.mean(distance, axis=1, keepdims=True)
         spread = jnp.mean(centered * centered, axis=1, keepdims=True)
         standardized = centered / jnp.sqrt(spread + 1e-06)
         members = softmax_rows(jnp.exp(-2.0 * standardized))
+        for route in routes:
+            score_copy(*route).wait_send()
         if it + 1 < ITERS:
-            put_members(members, mem1)
+            put_members(members, mem1, rows1)
         else:
             memb_out[...] = members
             std_out[...] = standardized
-        stream.finish()
+    for it in range(ITERS):
+        mems[it].finish()
+        for dy, dx in row_near + row_mid + row_far:
+            row_copy(it, dy, dx).wait_send()
     feats.finish()
 
 
@@ -369,21 +398,23 @@
             pltpu.VMEM((wide, width), BF16),
             pltpu.VMEM((wide, 2 * clusters), BF16),
             pltpu.VMEM((wide, 2 * clusters), BF16),
+            pltpu.VMEM((tall, 2 * clusters), BF16),
+            pltpu.VMEM((tall, 2 * clusters), BF16),
             pltpu.VMEM((tall, wide), BF16),
             pltpu.VMEM((tall, wide), BF16),
-            pltpu.VMEM((SUB, clusters), F32),
             pltpu.VMEM((tall, clusters), F32),
-            pltpu.VMEM((ITERS, 2, 2, 128, clusters), F32),
-            pltpu.VMEM((ITERS, 2, 2, SUB, clusters), F32),
-            pltpu.VMEM((ITERS, SUB, clusters), F32),
+            pltpu.VMEM((8, clusters), F32),
+            pltpu.VMEM((ITERS, 7, SUB, clusters), F32),
             pltpu.VMEM((ITERS, 32, 8, clusters), F32),
             dma((9,)),
             dma((24,)),
             dma((17,)),
             dma((ITERS, 24)),
             dma((ITERS, 17)),
-            dma((ITERS, 9)),
-            dma((ITERS, 9)),
+            dma((ITERS, 7)),
+            dma((ITERS, 7)),
+            dma((ITERS, 7)),
+            dma((ITERS, 7)),
             dma((ITERS, 3, 16)),
             dma((ITERS, 3, 16)),
         ],

time: 121 us -> 104 us (0.86)
  Pallas kernels: 117 us -> 100 us
    pallas_call x1, Pallas kernels: 117 us -> 100 us  [on_device(): pl.pallas_call(kernel, out_shape=(out, out), in_specs=[pl.BlockSpec(memor...]
where the time goes in v2:
time: 104 us
  Pallas kernels  100 us (96%)
  local copies, waits for them, and re-layouts  3.14 us (3%)
    pallas_call x1, Pallas kernels, on_device(): pl.pallas_call(kernel, out_shape=(out, out), in_specs=[pl.BlockSpec(memor...  100 us
    unnamed x2, local copies, waits for them, and re-layouts  3.14 us

profile of v2, /device:TPU:1, one launch (start us, length us, event | category | flops | bytes accessed | tf_op | source)
XLA Modules:
  0.0 104.2 jit_solution(15975554130306825125)
XLA Ops:
  0.6 100.5 %shard_map.41 = (f32[256,128]{1,0:T(8,128)}, f32[256,128]{1,0:T(8,128)}) custom-call(bf16[4096,512]{1,0:T(8,128)(2,1)} %feat.1, f32[256,128]{1,0:T(8,128)} %logits.1), custom_call_target="tpu_custom_call" | custom-call | tf_op jit(solution)/shard_map/pallas_call | solution.py:391
  101.1 1.6 %copy.6 = f32[256,128]{1,0:T(8,128)} copy(f32[256,128]{1,0:T(8,128)} %get-tuple-element.4) | data formatting | bytes 262144
  102.7 1.6 %copy.7 = f32[256,128]{1,0:T(8,128)} copy(f32[256,128]{1,0:T(8,128)} %get-tuple-element.5) | data formatting | bytes 262144

commit v3 on v2

--- a/solution.py
+++ b/solution.py
@@ -80,93 +80,61 @@
 
     class Stream:
         def __init__(self, buf, send, recv, own_src=None):
-            self.buf, self.send, self.recv = buf, send, recv
-            self.own_src = own_src
-            self.sent = 0
+            self.buf, self.send, self.recv, self.own_src = buf, send, recv, own_src
             self.started = []
 
         def at(self, slot, half=None, other=False):
-            part = 1 - core if other else core
-            start = slot * 2 * SUB + part * SUB
+            start = slot * 2 * SUB + (1 - core if other else core) * SUB
             if half is None:
                 return self.buf.at[rows(start)]
             return self.buf.at[rows(start + half * (SUB // 2), SUB // 2)]
 
-        def make(self, src, dst, where, sem):
-            n = self.sent
-            self.sent += 1
-            self.started.append((n, src))
-            return pltpu.make_async_remote_copy(
-                src_ref=src(), dst_ref=dst, send_sem=self.send.at[n], recv_sem=self.recv.at[sem],
-                device_id=where, device_id_type=MESH,
-            )
-
-        def wait(self, *sems):
-            for s in sems:
-                if s >= 9:
-                    dst = self.at(s - 9, other=True)
-                elif s >= 8:
-                    dst = self.at(7)
-                elif s >= 6 and self.own_src is not None:
-                    dst = self.at(6, s - 6)
+        def own(self, half=None):
+            if self.own_src is None:
+                return self.at(0, half)
+            start = self.own_src[1]
+            if half is None:
+                return self.own_src[0].at[rows(start)]
+            return self.own_src[0].at[rows(start + half * (SUB // 2), SUB // 2)]
+
+        def put(self, src, slot, where, half=None):
+            n = len(self.started)
+            self.started.append(src)
+            sem = 16 + slot if where is partner else 2 * slot + (half or 0)
+            pltpu.make_async_remote_copy(
+                src_ref=src(), dst_ref=self.at(slot, half), send_sem=self.send.at[n],
+                recv_sem=self.recv.at[sem], device_id=where, device_id_type=MESH,
+            ).start()
+
+        def wait(self, slot, half=None):
+            dst = self.at(slot, half)
+            pltpu.make_async_copy(dst, dst, self.recv.at[2 * slot + (half or 0)]).wait()
+
+        def ready(self, *slots):
+            for slot in slots:
+                dst = self.at(slot, other=True)
+                pltpu.make_async_copy(dst, dst, self.recv.at[16 + slot]).wait()
+
+        def pass_on(self, slot, *where):
+            for there, device_id in where:
+                self.put(lambda: self.at(slot), there, device_id)
+            self.put(lambda: self.at(slot), slot, partner)
+
+        def relay(self, *slots):
+            for slot in slots:
+                self.wait(slot)
+                if slot == 1:
+                    self.pass_on(1, (5, z_up), (6, z_down))
+                elif slot == 2:
+                    self.pass_on(2, (7, cross))
                 else:
-                    dst = self.at(s)
-                pltpu.make_async_copy(dst, dst, self.recv.at[s]).wait()
-
-        def send_own(self):
-            src = self.own_src or (lambda: self.at(0))
-            self.make(src, self.at(2), z_up, 2).start()
-            self.make(src, self.at(3), z_down, 3).start()
-            self.make(src, self.at(1), cross, 1).start()
-            if self.own_src is None:
-                self.make(src, self.at(0), partner, 9).start()
-
-        def to_partner(self, slot):
-            self.make(lambda: self.at(slot), self.at(slot), partner, 9 + slot).start()
-
-        def forward_1(self):
-            self.wait(1)
-            self.make(lambda: self.at(1), self.at(4), z_up, 4).start()
-            self.make(lambda: self.at(1), self.at(5), z_down, 5).start()
-            self.to_partner(1)
-
-        def send_far(self):
-            self.make(lambda: self.at(0), self.at(6), z_far, 6).start()
-
-        def forward_2(self):
-            self.wait(2)
-            if self.own_src is not None:
-                self.make(lambda: self.at(2, 0), self.at(6, 0), z_up, 6).start()
-            self.to_partner(2)
-
-        def forward_3(self):
-            self.wait(3)
-            if self.own_src is not None:
-                self.make(lambda: self.at(3, 1), self.at(6, 1), z_down, 7).start()
-            self.to_partner(3)
-
-        def forward_45(self):
-            self.wait(4)
-            self.to_partner(4)
-            self.wait(5)
-            self.to_partner(5)
-
-        def forward_6(self):
-            self.wait(6)
-            if self.own_src is not None:
-                self.wait(7)
-            self.make(lambda: self.at(6), self.at(7), cross, 8).start()
-            self.to_partner(6)
-
-        def forward_7(self):
-            self.wait(8)
-            self.to_partner(7)
+                    self.pass_on(slot)
 
         def finish(self):
-            for n, src in self.started:
+            for n, src in enumerate(self.started):
                 pltpu.make_async_copy(src(), src(), self.send.at[n]).wait()
 
-    feats = Stream(fcol, f_send, f_recv, lambda: feat.at[rows(col * SUB)])
+    feats = Stream(fcol, f_send, f_recv, (feat, col * SUB))
     mems = [Stream(mem, m_send.at[i], m_recv.at[i]) for i, mem in enumerate((mem0, mem1))]
 
     def row_copy(it, dy, dx):
@@ -188,8 +156,12 @@
 
     row_near, row_mid, row_far = [(1, 0), (3, 0), (0, 1)], [(2, 0), (1, 1), (3, 1)], [(2, 1)]
 
-    feats.send_own()
-    mems[0].send_own()
+    for first in range(2):
+        feats.put(lambda h=first: feats.own(h), 3, z_up, first)
+        feats.put(lambda h=1 - first: feats.own(h), 4, z_down, 1 - first)
+    feats.put(feats.own, 1, cross)
+    mems[0].put(mems[0].own, 0, partner)
+    mems[0].put(mems[0].own, 1, cross)
     send_rows(0, row_near)
 
     for load in loads:
@@ -231,26 +203,24 @@
 
         lax.fori_loop(0, 4, chunk, 0)
 
-    def exchange(members, buf, send, recv, group):
-        buf[0] = jnp.broadcast_to(members, buf.shape[1:])
-        copies = []
-        for j, (where, slot) in enumerate(group):
-            copies.append(
-                pltpu.make_async_remote_copy(
-                    src_ref=buf.at[0], dst_ref=buf.at[slot], send_sem=send.at[j],
-                    recv_sem=recv.at[slot], device_id=where, device_id_type=MESH,
-                )
+    def exchange(values, buf, send, recv, group):
+        buf[0] = values
+        copies = [
+            pltpu.make_async_remote_copy(
+                src_ref=buf.at[0], dst_ref=buf.at[slot], send_sem=send.at[slot],
+                recv_sem=recv.at[slot], device_id=where, device_id_type=MESH,
             )
-            copies[-1].start()
+            for where, slot in group
+        ]
+        for copy in copies:
+            copy.start()
 
         def finish():
-            for copy in copies:
+            out = buf[0]
+            for copy, (_, slot) in zip(copies, group):
+                pltpu.make_async_copy(buf.at[slot], buf.at[slot], recv.at[slot]).wait()
                 copy.wait_send()
-            for _, slot in group:
-                pltpu.make_async_copy(buf.at[slot], buf.at[slot], recv.at[slot]).wait()
-            out = buf[0, 0:1, :]
-            for _, slot in group:
-                out = out + buf[slot, 0:1, :]
+                out = out + buf[slot]
             return out
 
         return finish
@@ -262,61 +232,65 @@
 
     for it in range(ITERS):
         mem, stream, tile_rows = (mem0, mem1)[it], mems[it], (rows0, rows1)[it]
+        row_all = row_near + row_mid + row_far
         if it == 0:
             inner(0, 1)
-            stream.wait(9)
+            stream.ready(0)
             column_pass(mem, 0, 1)
-            feats.forward_2()
-            feats.forward_3()
-            feats.forward_1()
+            feats.wait(3, 0)
+            feats.put(lambda: feats.at(3, 0), 2, z_up, 0)
+            feats.wait(4, 1)
+            feats.put(lambda: feats.at(4, 1), 2, z_down, 1)
+            stream.put(stream.own, 2, z_far)
+            stream.put(stream.own, 3, z_up)
+            stream.put(stream.own, 4, z_down)
+            feats.relay(1)
+            for slot, half in ((3, 1), (4, 0)):
+                feats.wait(slot, half)
+                feats.pass_on(slot)
             wait_rows(0, row_near)
             send_rows(0, row_mid)
-            stream.send_far()
-            stream.forward_1()
-            feats.wait(10, 11, 12)
+            feats.ready(1)
             inner(1, 2)
-            stream.forward_2()
-            stream.forward_3()
+            feats.wait(2, 0)
+            feats.wait(2, 1)
+            feats.pass_on(2, (7, cross))
+            stream.relay(1)
+            feats.ready(3, 4)
+            inner(3, 5)
             wait_rows(0, row_mid)
             send_rows(0, row_far)
+            stream.relay(2)
+            feats.ready(2)
             inner(2, 3)
-            feats.forward_6()
-            inner(3, 4)
-            stream.wait(10, 11, 12)
-            column_pass(
-                mem, 1, 4,
-                [(0, feats.forward_45), (1, stream.forward_6), (2, stream.forward_45)],
-            )
-            feats.wait(13, 14)
-            inner(4, 5)
-            feats.forward_7()
+            stream.relay(3, 4)
+            stream.ready(1, 2)
+            column_pass(mem, 1, 3, [(3, lambda: feats.relay(7))])
+            stream.ready(3, 4)
+            column_pass(mem, 3, 5, [(2, lambda: feats.relay(5, 6))])
+            feats.ready(7)
+            inner(7, 8)
+            feats.ready(5, 6)
             inner(5, 6)
-            stream.forward_7()
-            feats.wait(15, 16)
-            inner(6, 8)
-            wait_rows(0, row_far)
+            stream.relay(7)
+            inner(6, 7)
+            stream.relay(5, 6)
         else:
-            stream.send_own()
-            stream.send_far()
-            send_rows(it, row_near + row_mid + row_far)
-            stream.wait(9)
+            stream.put(stream.own, 0, partner)
+            stream.put(stream.own, 2, z_far)
+            stream.put(stream.own, 1, cross)
+            stream.put(stream.own, 3, z_up)
+            stream.put(stream.own, 4, z_down)
+            send_rows(it, row_all)
+            stream.ready(0)
             column_pass(mem, 0, 1)
-            stream.forward_1()
-            stream.forward_2()
-            stream.forward_3()
-            stream.wait(10, 11, 12)
-            column_pass(mem, 1, 4, [(2, stream.forward_6), (3, stream.forward_45)])
-            wait_rows(it, row_near + row_mid + row_far)
-        stream.wait(13, 14)
-        column_pass(mem, 4, 6, [(3, stream.forward_7)] if it else ())
-        stream.wait(15, 16)
-
-        ones = jnp.ones((16, 8 * 2 * SUB), BF16)
-        panel = jnp.dot(ones, mem[...], preferred_element_type=F32)[0:1]
-        size_done = exchange(
-            panel[:, :clusters] + panel[:, clusters:], vec.at[it, pl.ds(0, 8)],
-            v_send.at[it, 0], v_recv.at[it, 0], near_ids,
-        )
+            stream.relay(1)
+            stream.ready(1)
+            column_pass(mem, 1, 2)
+            stream.relay(2, 3, 4)
+            stream.ready(2, 3, 4)
+            column_pass(mem, 2, 5, [(1, lambda: stream.relay(5, 6)), (3, lambda: stream.relay(7))])
+        stream.ready(5, 6, 7)
 
         def score_copy(u, slot, where):
             return pltpu.make_async_remote_copy(
@@ -328,35 +302,45 @@
         routes = [
             (0, 0, across), (2, 1, y_up), (3, 2, y_down), (4, 3, y_up), (5, 4, y_down), (1, 5, y_far), (6, 6, across),
         ]
+        def of(ref, at):
+            return ref[at, 0:clusters].astype(F32) + ref[at, clusters : 2 * clusters].astype(F32)
+
+        def fold(values):
+            return jnp.sum(values.reshape(SUB // 8, 8, clusters), axis=0)
+
+        wait_rows(it, row_far if it == 0 else row_all)
         wsum[...] = jnp.zeros_like(wsum)
 
         def step(u, carry):
             at = rows(u * SUB)
-            part = total[at, :] + product(at, slice(6 * 2 * SUB, 8 * 2 * SUB), mem)
+            part = total[at, :] + product(at, slice(5 * 2 * SUB, 8 * 2 * SUB), mem)
             total[at, :] = part
-            weights = tile_rows[at, 0:clusters].astype(F32) + tile_rows[at, clusters : 2 * clusters].astype(F32)
-            wsum[...] += jnp.sum((weights * part).reshape(SUB // 8, 8, clusters), axis=0)
+            wsum[...] += fold(of(tile_rows, at) * part)
             for v, slot, where in routes[:5]:
                 pl.when(u == v)(lambda v=v, slot=slot, where=where: score_copy(v, slot, where).start())
             return carry
 
         lax.fori_loop(0, 8, step, 0)
-        weighted_done = exchange(
-            jnp.sum(wsum[...], axis=0, keepdims=True), vec.at[it, pl.ds(8, 8)],
-            v_send.at[it, 1], v_recv.at[it, 1], near_ids,
+        sizes = fold(of(tile_rows, rows(7 * SUB)))
+        first = lax.broadcasted_iota(jnp.int32, (8, clusters), 0) == 0
+        sums_done = exchange(
+            jnp.where(
+                first, jnp.sum(wsum[...], axis=0, keepdims=True), jnp.sum(sizes, axis=0, keepdims=True)
+            ),
+            vec.at[it, pl.ds(0, 16)], v_send.at[it, 0], v_recv.at[it, 0], far_ids,
         )
         score_copy(*routes[0]).wait_recv()
         total[rows(SUB), :] = total[rows(SUB), :] + inbox[it, 0]
         score_copy(*routes[5]).start()
+        sums_done = exchange(
+            sums_done(), vec.at[it, pl.ds(16, 8)], v_send.at[it, 1], v_recv.at[it, 1], near_ids,
+        )
         score_copy(*routes[1]).wait_recv()
         score_copy(*routes[2]).wait_recv()
         total[rows(6 * SUB), :] = total[rows(6 * SUB), :] + inbox[it, 1] + inbox[it, 2]
         score_copy(*routes[6]).start()
-        weighted_done = exchange(
-            weighted_done(), vec.at[it, pl.ds(16, 16)], v_send.at[it, 2], v_recv.at[it, 2], far_ids,
-        )
-        size = size_done()
-        weighted = weighted_done()
+        sums = sums_done()
+        weighted, size = sums[0:1], sums[1:2]
         for route in routes[3:]:
             score_copy(*route).wait_recv()
         scores = total[rows(7 * SUB), :]
@@ -405,18 +389,18 @@
             pltpu.VMEM((tall, clusters), F32),
             pltpu.VMEM((8, clusters), F32),
             pltpu.VMEM((ITERS, 7, SUB, clusters), F32),
-            pltpu.VMEM((ITERS, 32, 8, clusters), F32),
+            pltpu.VMEM((ITERS, 24, 8, clusters), F32),
             dma((9,)),
             dma((24,)),
-            dma((17,)),
+            dma((24,)),
             dma((ITERS, 24)),
-            dma((ITERS, 17)),
+            dma((ITERS, 24)),
             dma((ITERS, 7)),
             dma((ITERS, 7)),
             dma((ITERS, 7)),
             dma((ITERS, 7)),
-            dma((ITERS, 3, 16)),
-            dma((ITERS, 3, 16)),
+            dma((ITERS, 2, 16)),
+            dma((ITERS, 2, 16)),
         ],
         compiler_params=pltpu.CompilerParams(
             collective_id=0, has_side_effects=True, vmem_limit_bytes=62 * 1024 * 1024

time: 104 us -> 90.1 us (0.87)
  Pallas kernels: 100 us -> 86.2 us
    pallas_call x1, Pallas kernels: 100 us -> 86.2 us  [on_device(): pl.pallas_call(kernel, out_shape=(out, out), in_specs=[pl.BlockSpec(memor...]
where the time goes in v3:
time: 90.1 us; the launch traced here: 90 us
  Pallas kernels  86.2 us (96%)
  local copies, waits for them, and re-layouts  3.14 us (3%)
    pallas_call x1, Pallas kernels, on_device(): pl.pallas_call(kernel, out_shape=(out, out), in_specs=[pl.BlockSpec(memor...  86.2 us
    unnamed x2, local copies, waits for them, and re-layouts  3.14 us

profile of v3, /device:TPU:1, one launch (start us, length us, event | category | flops | bytes accessed | tf_op | source)
XLA Modules:
  0.0 90.0 jit_solution(5698573138854451292)
XLA Ops:
  0.6 86.2 %shard_map.41 = (f32[256,128]{1,0:T(8,128)}, f32[256,128]{1,0:T(8,128)}) custom-call(bf16[4096,512]{1,0:T(8,128)(2,1)} %feat.1, f32[256,128]{1,0:T(8,128)} %logits.1), custom_call_target="tpu_custom_call" | custom-call | tf_op jit(solution)/shard_map/pallas_call | solution.py:375
  86.8 1.6 %copy.6 = f32[256,128]{1,0:T(8,128)} copy(f32[256,128]{1,0:T(8,128)} %get-tuple-element.4) | data formatting | bytes 262144
  88.4 1.6 %copy.7 = f32[256,128]{1,0:T(8,128)} copy(f32[256,128]{1,0:T(8,128)} %get-tuple-element.5) | data formatting | bytes 262144

commit v4 on v3

--- a/solution.py
+++ b/solution.py
@@ -51,7 +51,7 @@
     for where in nearest:
         pl.semaphore_signal(barrier, inc=1, device_id=where, device_id_type=MESH)
 
-    order = [(2, 1), (2, 0), (1, 1), (3, 1), (1, 0), (3, 0), (0, 1), (0, 0)]
+    order = [(2, 1), (1, 1), (3, 1), (1, 0), (3, 0), (2, 0), (0, 1), (0, 0)]
     loads = []
     for u, (dy, dx) in enumerate(order):
         block = ((y + dy) % 4) * 4 + ((xl + dx) % 2) * 2 + core
@@ -79,8 +79,9 @@
     pl.semaphore_wait(barrier, len(nearest))
 
     class Stream:
-        def __init__(self, buf, send, recv, own_src=None):
+        def __init__(self, buf, send, recv, halves, own_src=None):
             self.buf, self.send, self.recv, self.own_src = buf, send, recv, own_src
+            self.halves = halves
             self.started = []
 
         def at(self, slot, half=None, other=False):
@@ -115,6 +116,16 @@
                 dst = self.at(slot, other=True)
                 pltpu.make_async_copy(dst, dst, self.recv.at[16 + slot]).wait()
 
+        def send_round(self):
+            for first in range(2):
+                self.put(lambda h=first: self.own(h), 3, z_up, first)
+                self.put(lambda h=1 - first: self.own(h), 4, z_down, 1 - first)
+
+        def ring(self):
+            for slot, half, where in ((3, 0, z_up), (4, 1, z_down)):
+                self.wait(slot, half)
+                self.put(lambda slot=slot, half=half: self.at(slot, half), 2, where, half)
+
         def pass_on(self, slot, *where):
             for there, device_id in where:
                 self.put(lambda: self.at(slot), there, device_id)
@@ -122,7 +133,9 @@
 
         def relay(self, *slots):
             for slot in slots:
-                self.wait(slot)
+                if self.halves and slot == 2:
+                    self.wait(2, 0)
+                self.wait(slot, {2: 1, 3: 1, 4: 0}.get(slot) if self.halves else None)
                 if slot == 1:
                     self.pass_on(1, (5, z_up), (6, z_down))
                 elif slot == 2:
@@ -134,8 +147,8 @@
             for n, src in enumerate(self.started):
                 pltpu.make_async_copy(src(), src(), self.send.at[n]).wait()
 
-    feats = Stream(fcol, f_send, f_recv, (feat, col * SUB))
-    mems = [Stream(mem, m_send.at[i], m_recv.at[i]) for i, mem in enumerate((mem0, mem1))]
+    feats = Stream(fcol, f_send, f_recv, True, (feat, col * SUB))
+    mems = [Stream(mem, m_send.at[i], m_recv.at[i], i == 1) for i, mem in enumerate((mem0, mem1))]
 
     def row_copy(it, dy, dx):
         there = order.index(((4 - dy) % 4, dx))
@@ -156,9 +169,7 @@
 
     row_near, row_mid, row_far = [(1, 0), (3, 0), (0, 1)], [(2, 0), (1, 1), (3, 1)], [(2, 1)]
 
-    for first in range(2):
-        feats.put(lambda h=first: feats.own(h), 3, z_up, first)
-        feats.put(lambda h=1 - first: feats.own(h), 4, z_down, 1 - first)
+    feats.send_round()
     feats.put(feats.own, 1, cross)
     mems[0].put(mems[0].own, 0, partner)
     mems[0].put(mems[0].own, 1, cross)
@@ -237,24 +248,16 @@
             inner(0, 1)
             stream.ready(0)
             column_pass(mem, 0, 1)
-            feats.wait(3, 0)
-            feats.put(lambda: feats.at(3, 0), 2, z_up, 0)
-            feats.wait(4, 1)
-            feats.put(lambda: feats.at(4, 1), 2, z_down, 1)
-            stream.put(stream.own, 2, z_far)
+            feats.ring()
             stream.put(stream.own, 3, z_up)
             stream.put(stream.own, 4, z_down)
-            feats.relay(1)
-            for slot, half in ((3, 1), (4, 0)):
-                feats.wait(slot, half)
-                feats.pass_on(slot)
+            stream.put(stream.own, 2, z_far)
+            feats.relay(1, 3, 4)
             wait_rows(0, row_near)
             send_rows(0, row_mid)
             feats.ready(1)
             inner(1, 2)
-            feats.wait(2, 0)
-            feats.wait(2, 1)
-            feats.pass_on(2, (7, cross))
+            feats.relay(2)
             stream.relay(1)
             feats.ready(3, 4)
             inner(3, 5)
@@ -267,41 +270,42 @@
             stream.ready(1, 2)
             column_pass(mem, 1, 3, [(3, lambda: feats.relay(7))])
             stream.ready(3, 4)
-            column_pass(mem, 3, 5, [(2, lambda: feats.relay(5, 6))])
+            column_pass(mem, 3, 5, [(1, lambda: feats.relay(5, 6)), (3, lambda: stream.relay(7))])
             feats.ready(7)
             inner(7, 8)
+            stream.relay(5, 6)
             feats.ready(5, 6)
-            inner(5, 6)
-            stream.relay(7)
-            inner(6, 7)
-            stream.relay(5, 6)
+            inner(5, 7)
         else:
             stream.put(stream.own, 0, partner)
-            stream.put(stream.own, 2, z_far)
+            stream.send_round()
             stream.put(stream.own, 1, cross)
-            stream.put(stream.own, 3, z_up)
-            stream.put(stream.own, 4, z_down)
             send_rows(it, row_all)
             stream.ready(0)
             column_pass(mem, 0, 1)
-            stream.relay(1)
+            stream.ring()
+            stream.relay(1, 3, 4, 2)
             stream.ready(1)
             column_pass(mem, 1, 2)
-            stream.relay(2, 3, 4)
             stream.ready(2, 3, 4)
-            column_pass(mem, 2, 5, [(1, lambda: stream.relay(5, 6)), (3, lambda: stream.relay(7))])
+            column_pass(mem, 2, 5, [(1, lambda: stream.relay(5, 6)), (2, lambda: stream.relay(7))])
         stream.ready(5, 6, 7)
 
-        def score_copy(u, slot, where):
+        def score_copy(n):
+            u, slot, start, size, where = routes[n]
             return pltpu.make_async_remote_copy(
-                src_ref=total.at[rows(u * SUB)], dst_ref=inbox.at[it, slot],
-                send_sem=r_send.at[it, slot], recv_sem=r_recv.at[it, slot],
+                src_ref=total.at[rows(u * SUB + start, size)], dst_ref=inbox.at[it, slot, pl.ds(start, size)],
+                send_sem=r_send.at[it, n], recv_sem=r_recv.at[it, n],
                 device_id=where, device_id_type=MESH,
             )
 
+        half = SUB // 2
         routes = [
-            (0, 0, across), (2, 1, y_up), (3, 2, y_down), (4, 3, y_up), (5, 4, y_down), (1, 5, y_far), (6, 6, across),
+            (0, 0, 0, SUB, across), (1, 1, 0, SUB, y_up), (2, 2, 0, SUB, y_down),
+            (3, 3, 0, half, y_up), (4, 4, 0, half, y_down), (5, 5, 0, SUB, y_far), (6, 6, 0, SUB, across),
+            (3, 3, half, half, y_up), (4, 4, half, half, y_down),
         ]
+
         def of(ref, at):
             return ref[at, 0:clusters].astype(F32) + ref[at, clusters : 2 * clusters].astype(F32)
 
@@ -316,8 +320,8 @@
             part = total[at, :] + product(at, slice(5 * 2 * SUB, 8 * 2 * SUB), mem)
             total[at, :] = part
             wsum[...] += fold(of(tile_rows, at) * part)
-            for v, slot, where in routes[:5]:
-                pl.when(u == v)(lambda v=v, slot=slot, where=where: score_copy(v, slot, where).start())
+            for v in range(5):
+                pl.when(u == v)(lambda v=v: score_copy(v).start())
             return carry
 
         lax.fori_loop(0, 8, step, 0)
@@ -329,20 +333,22 @@
             ),
             vec.at[it, pl.ds(0, 16)], v_send.at[it, 0], v_recv.at[it, 0], far_ids,
         )
-        score_copy(*routes[0]).wait_recv()
-        total[rows(SUB), :] = total[rows(SUB), :] + inbox[it, 0]
-        score_copy(*routes[5]).start()
+        score_copy(0).wait_recv()
+        total[rows(5 * SUB), :] = total[rows(5 * SUB), :] + inbox[it, 0]
+        score_copy(5).start()
+        score_copy(1).wait_recv()
+        score_copy(2).wait_recv()
+        total[rows(6 * SUB), :] = total[rows(6 * SUB), :] + inbox[it, 1] + inbox[it, 2]
+        score_copy(6).start()
+        score_copy(7).start()
+        score_copy(8).start()
         sums_done = exchange(
             sums_done(), vec.at[it, pl.ds(16, 8)], v_send.at[it, 1], v_recv.at[it, 1], near_ids,
         )
-        score_copy(*routes[1]).wait_recv()
-        score_copy(*routes[2]).wait_recv()
-        total[rows(6 * SUB), :] = total[rows(6 * SUB), :] + inbox[it, 1] + inbox[it, 2]
-        score_copy(*routes[6]).start()
         sums = sums_done()
         weighted, size = sums[0:1], sums[1:2]
-        for route in routes[3:]:
-            score_copy(*route).wait_recv()
+        for n in range(3, 9):
+            score_copy(n).wait_recv()
         scores = total[rows(7 * SUB), :]
         for slot in range(3, 7):
             scores = scores + inbox[it, slot]
@@ -351,8 +357,8 @@
         spread = jnp.mean(centered * centered, axis=1, keepdims=True)
         standardized = centered / jnp.sqrt(spread + 1e-06)
         members = softmax_rows(jnp.exp(-2.0 * standardized))
-        for route in routes:
-            score_copy(*route).wait_send()
+        for n in range(9):
+            score_copy(n).wait_send()
         if it + 1 < ITERS:
             put_members(members, mem1, rows1)
         else:
@@ -397,8 +403,8 @@
             dma((ITERS, 24)),
             dma((ITERS, 7)),
             dma((ITERS, 7)),
-            dma((ITERS, 7)),
-            dma((ITERS, 7)),
+            dma((ITERS, 9)),
+            dma((ITERS, 9)),
             dma((ITERS, 2, 16)),
             dma((ITERS, 2, 16)),
         ],

time: 90.1 us -> 86.1 us (0.956)
  Pallas kernels: 86.2 us -> 82.2 us
    pallas_call x1, Pallas kernels: 86.2 us -> 82.2 us  [on_device(): pl.pallas_call(kernel, out_shape=(out, out), in_specs=[pl.BlockSpec(memor...]
where the time goes in v4:
time: 86.1 us; the launch traced here: 86 us
  Pallas kernels  82.2 us (95%)
  local copies, waits for them, and re-layouts  3.14 us (4%)
    pallas_call x1, Pallas kernels, on_device(): pl.pallas_call(kernel, out_shape=(out, out), in_specs=[pl.BlockSpec(memor...  82.2 us
    unnamed x2, local copies, waits for them, and re-layouts  3.14 us

profile of v4, /device:TPU:1, one launch (start us, length us, event | category | flops | bytes accessed | tf_op | source)
XLA Modules:
  0.0 86.0 jit_solution(15980160033047731066)
XLA Ops:
  0.6 82.2 %shard_map.41 = (f32[256,128]{1,0:T(8,128)}, f32[256,128]{1,0:T(8,128)}) custom-call(bf16[4096,512]{1,0:T(8,128)(2,1)} %feat.1, f32[256,128]{1,0:T(8,128)} %logits.1), custom_call_target="tpu_custom_call" | custom-call | tf_op jit(solution)/shard_map/pallas_call | solution.py:381
  82.8 1.6 %copy.6 = f32[256,128]{1,0:T(8,128)} copy(f32[256,128]{1,0:T(8,128)} %get-tuple-element.4) | data formatting | bytes 262144
  84.4 1.6 %copy.7 = f32[256,128]{1,0:T(8,128)} copy(f32[256,128]{1,0:T(8,128)} %get-tuple-element.5) | data formatting | bytes 262144

commit v5 on v4

--- a/solution.py
+++ b/solution.py
@@ -43,8 +43,8 @@
     z_up, z_down, z_far = device(dz=1), device(dz=3), device(dz=2)
     cross, partner = device(dx1=1), device(dk=1)
     y_up, y_down, y_far, across = device(dy=1), device(dy=3), device(dy=2), device(dx2=1)
-    reduce_group = [(dy, dx) for dy in range(4) for dx in range(2)][1:]
-    gather_group = [(dz, dx, dk) for dz in range(4) for dx in range(2) for dk in range(2)][1:]
+    reduce_group = [(2, 1), (2, 0), (1, 1), (3, 1), (1, 0), (3, 0), (0, 1)]
+    gather_group = [(dz, dx, dk) for dz in (2, 1, 3, 0) for dx in (1, 0) for dk in (1, 0)][:-1]
 
     barrier = pltpu.get_barrier_semaphore()
     nearest = (z_up, z_down, cross, partner, y_up, y_down, across)
@@ -214,6 +214,8 @@
 
         lax.fori_loop(0, 4, chunk, 0)
 
+    pending = []
+
     def exchange(values, buf, send, recv, group):
         buf[0] = values
         copies = [
@@ -225,12 +227,12 @@
         ]
         for copy in copies:
             copy.start()
+        pending.extend(copies)
 
         def finish():
             out = buf[0]
-            for copy, (_, slot) in zip(copies, group):
+            for _, slot in group:
                 pltpu.make_async_copy(buf.at[slot], buf.at[slot], recv.at[slot]).wait()
-                copy.wait_send()
                 out = out + buf[slot]
             return out
 
@@ -246,12 +248,12 @@
         row_all = row_near + row_mid + row_far
         if it == 0:
             inner(0, 1)
-            stream.ready(0)
-            column_pass(mem, 0, 1)
             feats.ring()
             stream.put(stream.own, 3, z_up)
             stream.put(stream.own, 4, z_down)
             stream.put(stream.own, 2, z_far)
+            stream.ready(0)
+            column_pass(mem, 0, 1)
             feats.relay(1, 3, 4)
             wait_rows(0, row_near)
             send_rows(0, row_mid)
@@ -359,6 +361,9 @@
         members = softmax_rows(jnp.exp(-2.0 * standardized))
         for n in range(9):
             score_copy(n).wait_send()
+        for copy in pending:
+            copy.wait_send()
+        pending.clear()
         if it + 1 < ITERS:
             put_members(members, mem1, rows1)
         else:

time: 86.1 us -> 86 us (level)
  no operation moved by 1% of the time
where the time goes in v5:
time: 86 us; the launch traced here: 85.9 us
  Pallas kernels  82.1 us (95%)
  local copies, waits for them, and re-layouts  3.14 us (4%)
    pallas_call x1, Pallas kernels, on_device(): pl.pallas_call(kernel, out_shape=(out, out), in_specs=[pl.BlockSpec(memor...  82.1 us
    unnamed x2, local copies, waits for them, and re-layouts  3.14 us

profile of v5, /device:TPU:1, one launch (start us, length us, event | category | flops | bytes accessed | tf_op | source)
XLA Modules:
  0.0 85.9 jit_solution(17343759412121741087)
XLA Ops:
  0.6 82.1 %shard_map.41 = (f32[256,128]{1,0:T(8,128)}, f32[256,128]{1,0:T(8,128)}) custom-call(bf16[4096,512]{1,0:T(8,128)(2,1)} %feat.1, f32[256,128]{1,0:T(8,128)} %logits.1), custom_call_target="tpu_custom_call" | custom-call | tf_op jit(solution)/shard_map/pallas_call | solution.py:386
  82.7 1.6 %copy.6 = f32[256,128]{1,0:T(8,128)} copy(f32[256,128]{1,0:T(8,128)} %get-tuple-element.4) | data formatting | bytes 262144
  84.3 1.6 %copy.7 = f32[256,128]{1,0:T(8,128)} copy(f32[256,128]{1,0:T(8,128)} %get-tuple-element.5) | data formatting | bytes 262144

commit v6 on v5

--- a/solution.py
+++ b/solution.py
@@ -17,7 +17,7 @@
 
 
 def softmax_rows(raised):
-    return raised / jnp.sum(raised, axis=1, keepdims=True)
+    return raised * (1.0 / jnp.sum(raised, axis=1, keepdims=True))
 
 
 def kernel(
@@ -354,10 +354,10 @@
         scores = total[rows(7 * SUB), :]
         for slot in range(3, 7):
             scores = scores + inbox[it, slot]
-        distance = weighted / (size * size) - 2.0 * scores / size
+        distance = weighted / (size * size) - scores * (2.0 / size)
         centered = distance - jnp.mean(distance, axis=1, keepdims=True)
         spread = jnp.mean(centered * centered, axis=1, keepdims=True)
-        standardized = centered / jnp.sqrt(spread + 1e-06)
+        standardized = centered * (1.0 / jnp.sqrt(spread + 1e-06))
         members = softmax_rows(jnp.exp(-2.0 * standardized))
         for n in range(9):
             score_copy(n).wait_send()

time: 86 us -> 86 us (level)
  no operation moved by 1% of the time
where the time goes in v6:
time: 86 us; the launch traced here: 85.9 us
  Pallas kernels  82.1 us (95%)
  local copies, waits for them, and re-layouts  3.14 us (4%)
    pallas_call x1, Pallas kernels, on_device(): pl.pallas_call(kernel, out_shape=(out, out), in_specs=[pl.BlockSpec(memor...  82.1 us
    unnamed x2, local copies, waits for them, and re-layouts  3.14 us

profile of v6, /device:TPU:1, one launch (start us, length us, event | category | flops | bytes accessed | tf_op | source)
XLA Modules:
  0.0 85.9 jit_solution(6212475898179402661)
XLA Ops:
  0.6 82.1 %shard_map.41 = (f32[256,128]{1,0:T(8,128)}, f32[256,128]{1,0:T(8,128)}) custom-call(bf16[4096,512]{1,0:T(8,128)(2,1)} %feat.1, f32[256,128]{1,0:T(8,128)} %logits.1), custom_call_target="tpu_custom_call" | custom-call | tf_op jit(solution)/shard_map/pallas_call | solution.py:386
  82.7 1.6 %copy.6 = f32[256,128]{1,0:T(8,128)} copy(f32[256,128]{1,0:T(8,128)} %get-tuple-element.4) | data formatting | bytes 262144
  84.3 1.6 %copy.7 = f32[256,128]{1,0:T(8,128)} copy(f32[256,128]{1,0:T(8,128)} %get-tuple-element.5) | data formatting | bytes 262144
